TPU v7x, 256 devices: a whole 4x4x8 slice. The times are simulated.
256 devices in a mesh: section: 4 (over x), tp: 16 (over y, z_hi, core), dp: 4 (over z_lo).
Axes of the slice: x: 4, y: 4, z: 8 (z_hi: 2, z_lo: 4; z = z_hi * 4 + z_lo), core: 2. Of those that a mesh axis runs over, the one named last changes fastest.
Arguments:
- responses: bfloat16 [2048, 8192], P(('section', 'tp'), 'dp'), may hold values from -6 to 6
- weights: bfloat16 [4, 8192, 16384], P('section', 'dp', 'tp'), may hold values from -0.0625 to 0.0625
- readout: float32 [4, 16384], P('section', 'tp'), may hold values from -0.09375 to 0.09375
- lengths: int32 [16], replicated, may hold values from 1 to 256, 2048 in all
- groups: int32 [16], replicated, may hold values from 0 to 3
Outputs:
- weight_grad: bfloat16 [4, 2048, 16384], P('dp', 'section', 'tp')
- policy_loss: float32 [], replicated
Inputs may be any that keep to these rules, and one draw needn't show every extreme that they name: The lengths add up to 2048; the longest response has exactly 256 tokens.
All inputs are finite; a program needn't handle non-finite values.
Results may differ from a plain program's by a relative error of at most 0.005.
Values may be sent and summed in bfloat16 or wider, within the bound.
A program may use at most 64 MiB of HBM per device.

v0:
```python
import jax
import jax.numpy as jnp
from jax import lax
from jax.sharding import PartitionSpec as P

kl_weight = 0.2


def from_root(block, axis, source):
    block = jnp.where(lax.axis_index(axis) == source, block, jnp.zeros_like(block))
    return lax.psum(block, axis)


def advantages(rewards, groups):
    same_group = (groups[:, None] == groups[None, :]).astype(jnp.float32)
    members = jnp.sum(same_group, axis=1)
    group_mean = jnp.sum(same_group * rewards[None, :], axis=1) / members
    spread = jnp.sum(same_group * (rewards[None, :] - group_mean[:, None]) ** 2, axis=1) / members
    return (rewards - group_mean) / jnp.sqrt(spread + 1.0)


def contract_rows(left, right):
    return lax.dot_general(
        left, right, (((0,), (0,)), ((), ())), preferred_element_type=jnp.float32
    )


def local(responses, weights, readout, lengths, groups):
    gathered = lax.all_gather(responses, ("section", "tp"), axis=0, tiled=True)
    weight_block = weights[0]
    total_rows = gathered.shape[0]
    row_block = total_rows // lax.axis_size("dp")
    hidden = lax.psum_scatter(
        jnp.dot(gathered, weight_block, preferred_element_type=jnp.float32),
        "dp",
        scatter_dimension=0,
        tiled=True,
    )
    read_row = readout[0]
    partial_score = jnp.sum(jax.nn.silu(hidden) * read_row[None, :], axis=1)
    own_score = lax.psum(partial_score, "tp")
    joined = lax.all_gather(own_score[None, :], "section", axis=0, tiled=True)
    resp_count = lengths.shape[0]
    first_row = lax.axis_index("dp") * row_block
    position = first_row + jnp.arange(row_block, dtype=jnp.int32)
    starts = jnp.cumsum(lengths) - lengths
    finish = starts + lengths
    in_response = (
        (position[:, None] >= starts[None, :]) & (position[:, None] < finish[None, :])
    ).astype(jnp.float32)
    last_token = (position[:, None] == finish[None, :] - 1).astype(jnp.float32)
    token_len = jnp.sum(in_response * lengths.astype(jnp.float32)[None, :], axis=1)
    lp_old = jax.nn.log_sigmoid(joined[0])
    lp_ref = jax.nn.log_sigmoid(joined[1])
    lp_new = jax.nn.log_sigmoid(joined[3])
    prob_ratio = jnp.exp(lp_new - lp_old)
    log_gap = lp_ref - lp_new
    penalty = kl_weight * (jnp.exp(log_gap) - log_gap - 1.0)
    reward_part = jnp.sum(last_token * joined[2][:, None], axis=0)
    rewards = lax.psum(reward_part, "dp")
    advantage = advantages(rewards, groups)
    token_adv = jnp.sum(in_response * advantage[None, :], axis=1)
    token_loss = -prob_ratio * token_adv + penalty
    policy_loss = lax.psum(jnp.sum(token_loss / token_len), "dp") / resp_count
    coeff = (
        total_rows
        / (resp_count * token_len)
        * (-prob_ratio * token_adv + kl_weight * (1.0 - jnp.exp(log_gap)))
        * jax.nn.sigmoid(-joined[3])
    )
    sigmoid_z = jax.nn.sigmoid(hidden)
    silu_slope = sigmoid_z * (1.0 + hidden * (1.0 - sigmoid_z))
    hidden_grad = (coeff[:, None] * read_row[None, :] * silu_slope).astype(jnp.bfloat16)
    block_width = gathered.shape[1] // lax.axis_size("section")
    feature_block = lax.dynamic_slice_in_dim(
        gathered, lax.axis_index("section") * block_width, block_width, 1
    )
    learner_index = lax.axis_size("section") - 1
    all_grad = lax.all_gather(hidden_grad, "dp", axis=0, tiled=True)
    shared_grad = from_root(all_grad, "section", learner_index)
    weight_grad = contract_rows(feature_block, shared_grad)
    return (weight_grad.astype(jnp.bfloat16)[None], policy_loss)


def solution(mesh):
    return jax.shard_map(
        local,
        mesh=mesh,
        in_specs=(
            P(("section", "tp"), "dp"),
            P("section", "dp", "tp"),
            P("section", "tp"),
            P(),
            P(),
        ),
        out_specs=(P("dp", "section", "tp"), P()),
        check_vma=False,
    )
```

profile of v0, /device:TPU:6, one launch (start us, length us, event | category | flops | bytes accessed | tf_op | source)
XLA Modules:
  0.0 554.7 jit_solution(10904170529704305852)
XLA Ops:
  7.2 0.7 all-gather.4.cloned.1.call-update
  7.9 117.6 %all-gather.4.cloned.1.call-done = bf16[2048,2048]{1,0:T(8,128)(2,1)} async-done(((bf16[32,2048]{1,0:T(8,128)(2,1)}), bf16[2048,2048]{1,0:T(8,128)(2,1)}) %all-gather.4.cloned.1.call-update) | async-done | bytes 8388624 | tf_op jit(solution)/shard_map/all_gather | solution.py:29
  125.6 14.4 %fusion = f32[2048,1024]{1,0:T(8,128)} fusion(bf16[2048,2048]{1,0:T(8,128)(2,1)} %all-gather.4.cloned.1.call-done, bf16[1,2048,1024]{2,1,0:T(8,128)(2,1)} %param.6), kind=kOutput, calls=%fused_computation | convolution fusion | flops 8589934592 | bytes 20971520 | tf_op jit(solution)/shard_map/dot_general | solution.py:34
  140.0 0.0 all-gather.6.cloned.1.call-start
  140.1 0.6 copy-done.3
  140.6 0.1 copy.10
  140.7 0.1 reduce
  140.9 144.6 %reduce-scatter.2.cloned.1.call-done = f32[512,1024]{1,0:T(8,128)} async-done(((f32[2048,1024]{1,0:T(8,128)}), f32[512,1024]{1,0:T(8,128)}) %reduce-scatter.2.cloned.1.call-update) | async-done | bytes 2097168 | tf_op jit(solution)/shard_map/reduce_scatter | solution.py:33
  285.5 2.4 multiply_reduce_fusion
  287.9 48.9 %psum.28 = f32[1,512]{1,0:T(1,128)S(1)} all-reduce(f32[1,512]{1,0:T(1,128)S(1)} %bitcast.22), channel_id=1, replica_groups=mesh['section'=4,'tp'=16,'dp'=4] {'tp'}, use_global_device_ids=true, to_apply=%region_4.5 | all-reduce | flops 512 | bytes 4096 | tf_op jit(solution)/shard_map/psum | solution.py:41
  336.8 10.1 %all-gather = f32[4,1,512]{2,1,0:T(1,128)S(1)} all-gather(f32[1,1,512]{2,1,0:T(1,128)S(1)} %bitcast.25), channel_id=1, replica_groups=mesh['section'=4,'tp'=16,'dp'=4] {'section'}, dimensions={0}, use_global_device_ids=true | all-gather | bytes 10240 | tf_op jit(solution)/shard_map/all_gather | solution.py:42
  346.9 0.2 select_reduce_fusion.1
  347.1 12.4 %psum.29 = f32[16]{0:T(128)S(1)} all-reduce(f32[16]{0:T(128)S(1)} %select_reduce_fusion.1), channel_id=1, replica_groups=mesh['section'=4,'tp'=16,'dp'=4] {'dp'}, use_global_device_ids=true, to_apply=%region_6.7 | all-reduce | flops 16 | bytes 128 | tf_op jit(solution)/shard_map/psum | solution.py:60
  359.6 0.2 fusion.11
  359.8 0.2 fusion.12
  360.0 0.1 select_reduce_fusion.2
  360.1 0.6 fusion.28
  360.7 1.8 multiply_convert_fusion
  362.5 0.0 all-reduce.2.cloned.1.call-start
  362.6 77.7 %all-gather.6.cloned.1.call-done = bf16[2048,1024]{1,0:T(8,128)(2,1)} async-done(((bf16[512,1024]{1,0:T(8,128)(2,1)}), bf16[2048,1024]{1,0:T(8,128)(2,1)}) %all-gather.6.cloned.1.call-update) | async-done | bytes 4194320 | tf_op jit(solution)/shard_map/all_gather | solution.py:79
  440.3 4.4 broadcast_select_fusion
  444.7 11.2 %psum.31 = f32[]{:T(128)} all-reduce(f32[]{:T(128)} %get-tuple-element.6), channel_id=1, replica_groups=mesh['section'=4,'tp'=16,'dp'=4] {'dp'}, use_global_device_ids=true, to_apply=%region_13.14 | all-reduce | flops 1 | bytes 8 | tf_op jit(solution)/shard_map/psum | solution.py:64
  456.6 84.3 %all-reduce.2.cloned.1.call-done = bf16[2048,1024]{1,0:T(8,128)(2,1)} async-done(((bf16[2048,1024]{1,0:T(8,128)(2,1)}), bf16[2048,1024]{1,0:T(8,128)(2,1)}) %all-reduce.2.cloned.1.call-update) | async-done | bytes 4194320 | tf_op jit(solution)/shard_map/psum | solution.py:11
  540.8 6.2 %fusion.7 = bf16[1,512,1024]{2,1,0:T(8,128)(2,1)} fusion(bf16[2048,1024]{1,0:T(8,128)(2,1)} %all-reduce.2.cloned.1.call-done, bf16[2048,2048]{1,0:T(8,128)(2,1)} %all-gather.4.cloned.1.call-done, s32[]{:T(128)S(6)} %select_n.34), kind=kOutput, calls=%fused_computation.9 | convolution fusion | flops 2148007936 | bytes 7340036 | tf_op jit(solution)/shard_map/dot_general | solution.py:23
  (19 shorter events, 0.2 us)
Async XLA Ops:
  7.2 118.4 %all-gather.4.cloned.1.call-start = ((), (), s32[]{:S(2)}) async-start(), calls=%async_computation.1 | async-start | bytes 8519680 | tf_op jit(solution)/shard_map/all_gather | solution.py:29
  7.9 277.6 %reduce-scatter.2.cloned.1.call-start = ((), (), s32[]{:S(2)}) async-start(), calls=%async_computation.2 | async-start | bytes 10485760 | tf_op jit(solution)/shard_map/reduce_scatter | solution.py:33
  140.0 0.7 copy-start.3
  140.0 145.6 %copy-start.1 = (f32[1,1024]{1,0:T(1,128)S(1)}, f32[1,1024]{1,0:T(1,128)}, u32[]{:S(2)}) copy-start(f32[1,1024]{1,0:T(1,128)} %param.7) | copy-start | bytes 12292
  140.0 219.6 %copy-start.2 = (s32[16]{0:T(128)S(1)}, s32[16]{0:T(128)}, u32[]{:S(2)}) copy-start(s32[16]{0:T(128)} %param.9) | copy-start | bytes 196
  140.0 300.3 %all-gather.6.cloned.1.call-start = ((), (), s32[]{:S(2)}) async-start(), calls=%async_computation.3 | async-start | bytes 5242880 | tf_op jit(solution)/shard_map/all_gather | solution.py:79
  285.5 75.2 %copy-start = (f32[512,1024]{1,0:T(8,128)S(1)}, f32[512,1024]{1,0:T(8,128)}, u32[]{:S(2)}) copy-start(f32[512,1024]{1,0:T(8,128)} %reduce-scatter.2.cloned.1.call-done) | copy-start | bytes 6291460
  362.5 178.3 %all-reduce.2.cloned.1.call-start = ((), (), s32[]{:S(2)}) async-start(), calls=%async_computation.4 | async-start | bytes 8388608 | tf_op jit(solution)/shard_map/psum | solution.py:11
Sparse Core Ops, SparseCore 0:
  11.5 114.0 all-gather.3
  140.1 145.3 reduce-scatter.1
  362.7 77.5 all-gather.5
  444.9 95.9 all-reduce.1
where the time goes:
time: 558 us; the launch traced here: 555 us
  waiting for transfers between devices  425 us (76%)
  blocking collectives  82.6 us (15%)
  matrix products  20.6 us (4%)
  between operations  15.6 us (3%)
  other arithmetic  10.1 us (2%)
    reduce_scatter x1, waiting for transfers between devices, local(): lax.psum_scatter(jnp.dot(gathered, weight_block, preferred_element_type=j...  145 us
    all_gather x1, waiting for transfers between devices, local(): gathered = lax.all_gather(responses, ('section', 'tp'), axis=0, tiled=True)  118 us
    psum x1, waiting for transfers between devices, from_root(): return lax.psum(block, axis)  84.3 us
    all_gather x1, waiting for transfers between devices, local(): all_grad = lax.all_gather(hidden_grad, 'dp', axis=0, tiled=True)  77.7 us
    psum x1, blocking collectives, local(): own_score = lax.psum(partial_score, 'tp')  48.9 us
    dot_general x1, matrix products, local(): jnp.dot(gathered, weight_block, preferred_element_type=jnp.float32)  14.4 us
    psum x1, blocking collectives, local(): rewards = lax.psum(reward_part, 'dp')  12.4 us
    psum x1, blocking collectives, local(): policy_loss = lax.psum(jnp.sum(token_loss / token_len), 'dp') / resp_count  11.2 us
  transfers between devices with their start and end apart: 4, of which 4 were waited for; matrix products, arithmetic and copies ran while one was open for 0% of the time, Pallas kernels for 0%

commit v1 on v0

v1 whole, which is shorter than its diff:
```python
import functools

import jax
import jax.numpy as jnp
from jax import lax
from jax.experimental import pallas as pl
from jax.experimental.pallas import tpu as pltpu
from jax.sharding import PartitionSpec as P

kl_weight = 0.2

RING = 4
SLOTS = 8
ROWS = 256
HALF = 128
SUB = 64
PIECE = 32
LAST = 3
Y_OFF = (0, 0, 3, 1, 3, 1, 2, 2)
H_OFF = (0, 1, 0, 0, 1, 1, 0, 1)


def wait_for(ref, sem):
    pltpu.make_async_copy(ref, ref, sem).wait()


def rows_at(start, size, step):
    return pl.ds(pl.multiple_of(start, step), size)


def slab_kernel(
    x_hbm, w_hbm, read_ref,
    score_ref, slope_out, feat_out,
    xg, wv, part_sum, landed, slope, lanes, score_rows, mine, peers, total, scores,
    local_sem, out_sem, gather_send, h_recv, x_recv, y_recv, sib_recv,
    sum_send, sum_recv, scat_send, scat_recv, line_send, line_recv,
    ring_send, ring_recv, peer_send, peer_recv, score_send, score_recv,
):
    sec = lax.axis_index("section")
    tp = lax.axis_index("tp")
    d = lax.axis_index("dp")
    y = tp // 4
    h = lax.rem(tp // 2, 2)
    c = lax.rem(tp, 2)

    def tp_at(y_, h_, c_):
        return (y_ * 2 + h_) * 2 + c_

    def ring(at, by):
        return lax.rem(at + by, RING)

    right, left = ring(sec, 1), ring(sec, 3)
    up, down = tp_at(ring(y, 1), h, c), tp_at(ring(y, 3), h, c)
    sibling = tp_at(y, h, 1 - c)
    far = tp_at(y, 1 - h, c)

    load_w = pltpu.make_async_copy(w_hbm.at[0], wv, local_sem.at[0])
    load_w.start()

    barrier = pltpu.get_barrier_semaphore()
    for k in range(1, 16):
        pl.semaphore_signal(
            barrier, inc=1,
            device_id={"section": sec, "tp": lax.rem(tp + k, 16), "dp": d},
            device_id_type=pl.DeviceIdType.MESH,
        )
    for k in range(1, 16):
        pl.semaphore_signal(
            barrier, inc=1,
            device_id={"section": ring(sec, k // 4), "tp": tp, "dp": ring(d, k % 4)},
            device_id_type=pl.DeviceIdType.MESH,
        )
    pl.semaphore_wait(barrier, 30)

    def push(src, dst, send_sem, recv_sem, sec_=None, tp_=None, d_=None):
        pltpu.make_async_remote_copy(
            src_ref=src, dst_ref=dst, send_sem=send_sem, recv_sem=recv_sem,
            device_id={
                "section": sec if sec_ is None else sec_,
                "tp": tp if tp_ is None else tp_,
                "dp": d if d_ is None else d_,
            },
            device_id_type=pl.DeviceIdType.MESH,
        ).start()

    origin = (sec, left, right, ring(sec, 2))

    def piece(slot, p, core):
        return xg.at[rows_at(slot * ROWS + origin[p] * SUB + core * PIECE, PIECE, PIECE)]

    def send_piece(src, slot, p, recv_sem, **to):
        push(src, piece(slot, p, c), gather_send, recv_sem, **to)

    def spread(slot, p, src):
        send_piece(src, (2, 4)[slot], p, y_recv.at[(2, 4)[slot], p], tp_=up)
        send_piece(src, (3, 5)[slot], p, y_recv.at[(3, 5)[slot], p], tp_=down)
        send_piece(src, slot, p, sib_recv.at[slot, p], tp_=sibling)

    own = pltpu.make_async_copy(x_hbm, piece(0, 0, c), local_sem.at[1])
    own.start()
    send_piece(x_hbm, 0, 0, x_recv.at[0, 0], sec_=right)
    send_piece(x_hbm, 0, 0, x_recv.at[0, 1], sec_=left)
    send_piece(x_hbm, 1, 0, h_recv, tp_=far)
    spread(0, 0, x_hbm)

    wait_for(piece(0, 1, c), x_recv.at[0, 0])
    send_piece(piece(0, 1, c), 0, 1, x_recv.at[0, 2], sec_=right)
    spread(0, 1, piece(0, 1, c))
    wait_for(piece(0, 2, c), x_recv.at[0, 1])
    spread(0, 2, piece(0, 2, c))
    wait_for(piece(0, 3, c), x_recv.at[0, 2])
    spread(0, 3, piece(0, 3, c))
    own.wait()
    load_w.wait()

    def second_block():
        wait_for(piece(1, 0, c), h_recv)
        send_piece(piece(1, 0, c), 1, 0, x_recv.at[1, 0], sec_=right)
        send_piece(piece(1, 0, c), 1, 0, x_recv.at[1, 1], sec_=left)
        spread(1, 0, piece(1, 0, c))
        wait_for(piece(1, 2, c), x_recv.at[1, 1])
        send_piece(piece(1, 2, c), 1, 2, x_recv.at[1, 2], sec_=left)
        spread(1, 2, piece(1, 2, c))
        wait_for(piece(1, 1, c), x_recv.at[1, 0])
        spread(1, 1, piece(1, 1, c))
        wait_for(piece(1, 3, c), x_recv.at[1, 2])
        spread(1, 3, piece(1, 3, c))

    def later_block(slot):
        for p in range(RING):
            wait_for(piece(slot, p, c), y_recv.at[slot, p])
            send_piece(piece(slot, p, c), slot, p, sib_recv.at[slot, p], tp_=sibling)

            @pl.when(slot == 2)
            def _():
                send_piece(piece(2, p, c), 6, p, y_recv.at[6, p], tp_=up)

            @pl.when(slot == 5)
            def _():
                send_piece(piece(5, p, c), 7, p, y_recv.at[7, p], tp_=down)

    def project(slot):
        for p in range(RING):
            wait_for(piece(slot, p, 1 - c), sib_recv.at[slot, p])
        block = rows_at(slot * ROWS, ROWS, ROWS)
        pltpu.make_async_copy(
            xg.at[block, rows_at(sec * 512, 512, 128)], feat_out.at[block], out_sem.at[0]
        ).start()
        for n in range(0, wv.shape[1], 256):
            part_sum[block, n:n + 256] = jnp.dot(
                xg[block, :], wv[:, n:n + 256], preferred_element_type=jnp.float32
            )

    def finish(start, slot, a):
        def some(t, carry):
            at = rows_at(start + t * 16, 16, 16)
            hidden = part_sum[at, :] + landed[at, :]
            gate = jax.nn.sigmoid(hidden)
            term = hidden * gate * read_ref[...]
            folded = term[:, 0:128]
            for n in range(128, term.shape[1], 128):
                folded = folded + term[:, n:n + 128]
            lanes[rows_at(a * SUB + t * 16, 16, 16), :] = folded

            @pl.when(sec == LAST)
            def _():
                slope[at, :] = (
                    read_ref[...] * gate * (1.0 + hidden * (1.0 - gate))
                ).astype(jnp.bfloat16)

            return carry

        lax.fori_loop(0, SUB // 16, some, 0)
        if a == 1:
            score_rows[pl.ds(slot, 1), :] = jnp.sum(
                jnp.transpose(lanes[...]), axis=0, keepdims=True
            )

    def add_up(i, half, a):
        hop = d if half == 1 else LAST - d
        onward = d + 1 if half == 1 else d - 1
        slot = i - hop
        start = slot * ROWS + half * HALF + a * SUB

        @pl.when((slot >= 0) & (slot < SLOTS))
        def _():
            at = rows_at(start, SUB, SUB)
            count = slot * 2 + a

            @pl.when(hop > 0)
            def _():
                wait_for(landed.at[at], sum_recv.at[half, count])

            @pl.when((hop > 0) & (hop < LAST))
            def _():
                part_sum[at, :] = part_sum[at, :] + landed[at, :]

            @pl.when(hop < LAST)
            def _():
                push(
                    part_sum.at[at], landed.at[at], sum_send.at[half],
                    sum_recv.at[half, count], d_=onward,
                )

            @pl.when(hop == LAST)
            def _():
                finish(start, slot, a)

    def quarter(slot, half, q):
        return slope.at[rows_at(slot * ROWS + half * HALF + q * PIECE, PIECE, PIECE)]

    def in_range(slot):
        return (slot >= 0) & (slot < SLOTS)

    def hand_on(i, half):
        hop = d if half == 0 else LAST - d
        onward = d + 1 if half == 0 else d - 1
        source = (hop == 0) & (sec == LAST)
        no_right = (hop == 0) & (sec == LAST - 1)
        no_left = (hop == 0) & (sec == 0)

        fresh = i - 3

        @pl.when(source & in_range(fresh))
        def _():
            for q in range(LAST):
                push(
                    quarter(fresh, half, q), quarter(fresh, half, q),
                    scat_send.at[half], scat_recv.at[half, fresh], sec_=q,
                )

        slot = i - 4 - hop

        @pl.when(in_range(slot))
        def _():
            held = quarter(slot, half, sec)

            @pl.when((hop == 0) & (sec < LAST))
            def _():
                wait_for(held, scat_recv.at[half, slot])

            @pl.when(hop > 0)
            def _():
                wait_for(held, line_recv.at[half, slot])

            @pl.when(hop < LAST)
            def _():
                push(held, held, line_send.at[half], line_recv.at[half, slot], d_=onward)

            @pl.when(jnp.logical_not(no_right))
            def _():
                push(held, held, ring_send.at[half], ring_recv.at[half, slot, 0], sec_=right)

            @pl.when(jnp.logical_not(no_left))
            def _():
                push(held, held, ring_send.at[half], ring_recv.at[half, slot, 1], sec_=left)

        slot1 = i - 5 - hop

        @pl.when(in_range(slot1))
        def _():
            from_left = quarter(slot1, half, left)
            from_right = quarter(slot1, half, right)

            @pl.when(jnp.logical_not(source))
            def _():
                wait_for(from_left, ring_recv.at[half, slot1, 0])
                wait_for(from_right, ring_recv.at[half, slot1, 1])

            if half == 0:
                @pl.when(jnp.logical_not(no_right))
                def _():
                    push(
                        from_left, from_left, ring_send.at[half],
                        ring_recv.at[half, slot1, 2], sec_=right,
                    )
            else:
                @pl.when(jnp.logical_not(no_left))
                def _():
                    push(
                        from_right, from_right, ring_send.at[half],
                        ring_recv.at[half, slot1, 2], sec_=left,
                    )

        slot2 = i - 6 - hop

        @pl.when(in_range(slot2))
        def _():
            @pl.when(jnp.logical_not(source))
            def _():
                wait_for(quarter(slot2, half, origin[3]), ring_recv.at[half, slot2, 2])

            at = rows_at(slot2 * ROWS + half * HALF, HALF, HALF)
            pltpu.make_async_copy(slope.at[at], slope_out.at[at], out_sem.at[1]).start()

    is_end = (d == 0) | (d == LAST)
    which = d // LAST

    def share_terms():
        for slot in range(SLOTS):
            row = ring(y, Y_OFF[slot]) * 2 + lax.rem(h + H_OFF[slot], 2)
            mine[pl.ds(row, 1), :] = score_rows[slot:slot + 1, :]
        for k in range(1, 16):
            push(mine, peers.at[tp], peer_send, peer_recv, tp_=lax.rem(tp + k, 16))
        peers[tp] = mine[...]

    def share_scores():
        wait_for(scores_like_peers(15), peer_recv)
        summed = peers[0]
        for k in range(1, 16):
            summed = summed + peers[k]
        total[...] = summed
        for k in range(1, 16):
            push(
                total, scores.at[sec * 2 + which], score_send, score_recv,
                sec_=ring(sec, k // 4), d_=ring(d, k % 4),
            )
        scores[sec * 2 + which] = summed

    def scores_like_peers(n):
        return peers.at[0:n]

    def step(i, carry):
        @pl.when(i < SLOTS)
        def _():
            project(i)

        for a in range(2):
            add_up(i, 1, a)
            add_up(i, 0, a)

        @pl.when(i == 0)
        def _():
            second_block()

        @pl.when((i >= 1) & (i < SLOTS - 1))
        def _():
            later_block(i + 1)

        @pl.when((i == 10) & is_end)
        def _():
            share_terms()

        hand_on(i, 0)
        hand_on(i, 1)

        @pl.when((i == 12) & is_end)
        def _():
            share_scores()

        return carry

    lax.fori_loop(0, SLOTS + 9, step, 0)

    @pl.when(is_end)
    def _():
        wait_for(scores.at[0:7], score_recv)

    @pl.when(jnp.logical_not(is_end))
    def _():
        wait_for(scores.at[0:8], score_recv)

    score_ref[...] = scores[...]

    wait_for(xg.at[0:63 * PIECE], gather_send)
    for half in range(2):
        sum_hop = d if half == 1 else LAST - d
        hop = d if half == 0 else LAST - d
        source = (hop == 0) & (sec == LAST)
        one = (hop == 0) & (sec == (LAST - 1 if half == 0 else 0))
        two = (hop == 0) & (sec == (0 if half == 0 else LAST - 1))

        @pl.when(sum_hop < LAST)
        def _():
            wait_for(part_sum.at[0:SLOTS * HALF], sum_send.at[half])

        @pl.when(source)
        def _():
            wait_for(slope.at[0:3 * SLOTS * PIECE], scat_send.at[half])

        @pl.when(hop < LAST)
        def _():
            wait_for(slope.at[0:SLOTS * PIECE], line_send.at[half])

        @pl.when(one)
        def _():
            wait_for(slope.at[0:SLOTS * PIECE], ring_send.at[half])

        @pl.when(two)
        def _():
            wait_for(slope.at[0:2 * SLOTS * PIECE], ring_send.at[half])

        @pl.when(jnp.logical_not(one | two))
        def _():
            wait_for(slope.at[0:3 * SLOTS * PIECE], ring_send.at[half])

    @pl.when(is_end)
    def _():
        wait_for(scores_like_peers(15), peer_send)
        wait_for(scores_like_peers(15), score_send)

    wait_for(feat_out, out_sem.at[0])
    wait_for(slope_out, out_sem.at[1])


def score_and_slope(responses, weights, readout):
    tokens, width, units = ROWS * SLOTS, weights.shape[1], weights.shape[2]
    block_width = width // RING
    dma = pltpu.SemaphoreType.DMA
    any_space = pl.BlockSpec(memory_space=pl.ANY)
    in_vmem = pl.BlockSpec(memory_space=pltpu.VMEM)
    return pl.pallas_call(
        slab_kernel,
        out_shape=(
            jax.ShapeDtypeStruct((8, 8, 128), jnp.float32),
            jax.ShapeDtypeStruct((tokens, units), jnp.bfloat16),
            jax.ShapeDtypeStruct((tokens, block_width), jnp.bfloat16),
        ),
        in_specs=[any_space, any_space, in_vmem],
        out_specs=(in_vmem, any_space, any_space),
        scratch_shapes=[
            pltpu.VMEM((tokens, width), jnp.bfloat16),
            pltpu.VMEM((width, units), jnp.bfloat16),
            pltpu.VMEM((tokens, units), jnp.float32),
            pltpu.VMEM((tokens, units), jnp.float32),
            pltpu.VMEM((tokens, units), jnp.bfloat16),
            pltpu.VMEM((128, 128), jnp.float32),
            pltpu.VMEM((8, 128), jnp.float32),
            pltpu.VMEM((8, 128), jnp.float32),
            pltpu.VMEM((16, 8, 128), jnp.float32),
            pltpu.VMEM((8, 128), jnp.float32),
            pltpu.VMEM((8, 8, 128), jnp.float32),
            dma((2,)), dma((2,)), dma, dma, dma((2, 3)), dma((8, 4)), dma((8, 4)),
            dma((2,)), dma((2, 16)), dma((2,)), dma((2, 8)), dma((2,)), dma((2, 8)),
            dma((2,)), dma((2, 8, 3)), dma, dma, dma, dma,
        ],
        compiler_params=pltpu.CompilerParams(
            collective_id=0, has_side_effects=True, vmem_limit_bytes=50 * 1024 * 1024,
        ),
        name="score_and_slope",
    )(responses, weights, readout)


def advantages(rewards, groups):
    same_group = (groups[:, None] == groups[None, :]).astype(jnp.float32)
    members = jnp.sum(same_group, axis=1)
    group_mean = jnp.sum(same_group * rewards[None, :], axis=1) / members
    spread = jnp.sum(same_group * (rewards[None, :] - group_mean[:, None]) ** 2, axis=1) / members
    return (rewards - group_mean) / jnp.sqrt(spread + 1.0)


def contract_rows(left, right):
    return lax.dot_general(
        left, right, (((0,), (0,)), ((), ())), preferred_element_type=jnp.float32
    )


def local(responses, weights, readout, lengths, groups):
    scores, slope, features = score_and_slope(responses, weights, readout)
    total_rows = slope.shape[0]
    resp_count = lengths.shape[0]
    joined = scores.reshape(RING, total_rows)
    shape = (2, 4, 2, 2, SUB)
    half, at_y, at_h, at_x, inner = (
        lax.broadcasted_iota(jnp.int32, shape, n) for n in range(5)
    )
    position = (((half * 2 + at_x) * 4 + at_y) * 2 + at_h) * SUB + inner
    position = position.reshape(total_rows)
    starts = jnp.cumsum(lengths) - lengths
    finish = starts + lengths
    in_response = (
        (position[:, None] >= starts[None, :]) & (position[:, None] < finish[None, :])
    ).astype(jnp.float32)
    last_token = (position[:, None] == finish[None, :] - 1).astype(jnp.float32)
    token_len = jnp.sum(in_response * lengths.astype(jnp.float32)[None, :], axis=1)
    lp_old = jax.nn.log_sigmoid(joined[0])
    lp_ref = jax.nn.log_sigmoid(joined[1])
    lp_new = jax.nn.log_sigmoid(joined[3])
    prob_ratio = jnp.exp(lp_new - lp_old)
    log_gap = lp_ref - lp_new
    penalty = kl_weight * (jnp.exp(log_gap) - log_gap - 1.0)
    rewards = jnp.sum(last_token * joined[2][:, None], axis=0)
    advantage = advantages(rewards, groups)
    token_adv = jnp.sum(in_response * advantage[None, :], axis=1)
    token_loss = -prob_ratio * token_adv + penalty
    policy_loss = jnp.sum(token_loss / token_len) / resp_count
    coeff = (
        total_rows
        / (resp_count * token_len)
        * (-prob_ratio * token_adv + kl_weight * (1.0 - jnp.exp(log_gap)))
        * jax.nn.sigmoid(-joined[3])
    )
    tp = lax.axis_index("tp")
    block = (
        lax.rem(tp // 4 + jnp.array(Y_OFF, jnp.int32), 4) * 2
        + lax.rem(tp // 2 + jnp.array(H_OFF, jnp.int32), 2)
    )
    by_block = coeff.reshape(2, SLOTS, HALF).transpose(1, 0, 2).reshape(SLOTS, ROWS)
    ordered = jnp.take(by_block, block, axis=0).reshape(total_rows)
    hidden_grad = ordered[:, None] * slope.astype(jnp.float32)
    upper = hidden_grad.astype(jnp.bfloat16)
    lower = (hidden_grad - upper.astype(jnp.float32)).astype(jnp.bfloat16)
    weight_grad = contract_rows(features, upper) + contract_rows(features, lower)
    return (weight_grad.astype(jnp.bfloat16)[None], policy_loss)


def solution(mesh):
    return jax.shard_map(
        local,
        mesh=mesh,
        in_specs=(
            P(("section", "tp"), "dp"),
            P("section", "dp", "tp"),
            P("section", "tp"),
            P(),
            P(),
        ),
        out_specs=(P("dp", "section", "tp"), P()),
        check_vma=False,
    )
```

time: 558 us -> 185 us (0.33)
  waiting for transfers between devices: 425 us -> 0 us
  Pallas kernels: 0 us -> 168 us
  blocking collectives: 82.6 us -> 0 us
  between operations: 15.6 us -> 2.51 us
  matrix products: 20.6 us -> 8.35 us
  other arithmetic: 10.1 us -> 3.1 us
    all_gather x2 -> x0, waiting for transfers between devices: 195 us -> none  [the longest x1 118 us: local(): gathered = lax.all_gather(responses, ('section', 'tp'), axis=0, tiled=True)]
    pallas_call x0 -> x1, Pallas kernels: none -> 168 us  [score_and_slope(): pl.pallas_call(slab_kernel, out_shape=(jax.ShapeDtypeStruct((8, 8, 128),...]
    reduce_scatter x1 -> x0, waiting for transfers between devices: 145 us -> none  [local(): lax.psum_scatter(jnp.dot(gathered, weight_block, preferred_element_type=j...]
    psum x1 -> x0, waiting for transfers between devices: 84.3 us -> none  [from_root(): return lax.psum(block, axis)]
    psum x3 -> x0, blocking collectives: 72.5 us -> none  [the longest x1 48.9 us: local(): own_score = lax.psum(partial_score, 'tp')]
    dot_general x1 -> x0, matrix products: 14.4 us -> none  [local(): jnp.dot(gathered, weight_block, preferred_element_type=jnp.float32)]
    all_gather x1 -> x0, blocking collectives: 10.1 us -> none  [local(): joined = lax.all_gather(own_score[None, :], 'section', axis=0, tiled=True)]
  transfers between devices with their start and end apart: 4 -> 0, of which waited for: 4 -> 0; matrix products, arithmetic and copies ran while one was open for 0% -> 0% of each run, Pallas kernels for 0% -> 0%
where the time goes in v1:
time: 185 us
  Pallas kernels  168 us (91%)
  matrix products  8.35 us (5%)
  other arithmetic  3.1 us (2%)
  local copies, waits for them, and re-layouts  2.99 us (2%)
  between operations  2.51 us (1%)
    pallas_call x1, Pallas kernels, score_and_slope(): pl.pallas_call(slab_kernel, out_shape=(jax.ShapeDtypeStruct((8, 8, 128),...  168 us
    dot_general x2, matrix products, contract_rows(): lax.dot_general(left, right, (((0,), (0,)), ((), ())), preferred_element_...  8.35 us

profile of v1, /device:TPU:6, one launch (start us, length us, event | category | flops | bytes accessed | tf_op | source)
XLA Modules:
  0.0 184.6 jit_solution(12036907429820846226)
XLA Ops:
  0.6 0.0 copy-start.2
  0.7 0.7 compare_and_fusion.1
  1.4 0.7 copy.11
  2.1 0.1 reduce.1
  2.3 0.7 fusion.33
  3.0 0.1 multiply_add_fusion
  3.1 0.1 reshape.138
  3.2 0.0 copy-start
  3.2 0.9 copy-done
  4.1 0.0 copy-start.1
  4.1 0.7 copy-done.1
  4.8 167.7 %score_and_slope.1 = (f32[8,8,128]{2,1,0:T(8,128)S(1)}, bf16[2048,1024]{1,0:T(8,128)(2,1)}, bf16[2048,512]{1,0:T(8,128)(2,1)S(1)}) custom-call(bf16[32,2048]{1,0:T(8,128)(2,1)S(1)} %copy-done, bf16[1,2048,1024]{2,1,0:T(8,128)(2,1)} %w_hbm.1, f32[1,1024]{1,0:T(1,128)S(1)} %copy-done.1), custom_call_target="tpu_custom_call" | custom-call | tf_op jit(solution)/shard_map/score_and_slope/pallas_call | solution.py:412
  172.5 0.2 select_reduce_fusion.1
  172.7 0.0 copy-done.2
  172.7 0.2 fusion.17
  172.8 0.2 fusion.18
  173.1 0.1 select_reduce_fusion
  173.2 0.6 fusion.28
  174.5 0.6 gather_fusion
  175.1 0.1 select_bitcast_fusion
  175.1 0.0 copy-start.3
  175.1 4.9 %fusion.1 = f32[512,1024]{1,0:T(8,128)S(1)} fusion(bf16[2048,512]{1,0:T(8,128)(2,1)S(1)} %get-tuple-element.5, bf16[2048,1024]{1,0:T(8,128)(2,1)} %get-tuple-element.7, f32[2048]{0:T(1024)S(1)} %bitcast.29), kind=kOutput, calls=%fused_computation.4 | convolution fusion | flops 2153775104 | bytes 8396800 | tf_op jit(solution)/shard_map/dot_general | solution.py:453
  180.0 0.0 copy-done.3
  180.0 3.5 %fusion.6 = bf16[1,512,1024]{2,1,0:T(8,128)(2,1)} fusion(f32[512,1024]{1,0:T(8,128)S(1)} %fusion.1, bf16[2048,512]{1,0:T(8,128)(2,1)S(1)} %get-tuple-element.5, bf16[2048,1024]{1,0:T(8,128)(2,1)S(1)} %copy-done.3, f32[2048]{0:T(1024)S(1)} %bitcast.30), kind=kOutput, calls=%fused_computation.9 | convolution fusion | flops 2161115136 | bytes 9445376 | tf_op jit(solution)/shard_map/dot_general | solution.py:453
  (7 shorter events, 0.1 us)
Async XLA Ops:
  0.6 172.0 %copy-start.2 = (s32[16]{0:T(128)S(1)}, s32[16]{0:T(128)}, u32[]{:S(2)}) copy-start(s32[16]{0:T(128)} %param.11) | copy-start | bytes 196
  3.2 0.9 copy-start
  4.1 0.7 copy-start.1
  175.1 4.9 %copy-start.3 = (bf16[2048,1024]{1,0:T(8,128)(2,1)S(1)}, bf16[2048,1024]{1,0:T(8,128)(2,1)}, u32[]{:S(2)}) copy-start(bf16[2048,1024]{1,0:T(8,128)(2,1)} %get-tuple-element.7) | copy-start | bytes 12582916

commit v2 on v1

--- a/solution.py
+++ b/solution.py
@@ -16,6 +16,7 @@
 SUB = 64
 PIECE = 32
 LAST = 3
+STEPS = 32767.0
 Y_OFF = (0, 0, 3, 1, 3, 1, 2, 2)
 H_OFF = (0, 1, 0, 0, 1, 1, 0, 1)
 
@@ -31,9 +32,9 @@
 def slab_kernel(
     x_hbm, w_hbm, read_ref,
     score_ref, slope_out, feat_out,
-    xg, wv, part_sum, landed, slope, lanes, score_rows, mine, peers, total, scores,
+    xg, wv, part_sum, sent, landed, unit_sent, unit_landed, slope, lanes, score_rows, mine, peers, total, scores,
     local_sem, out_sem, gather_send, h_recv, x_recv, y_recv, sib_recv,
-    sum_send, sum_recv, scat_send, scat_recv, line_send, line_recv,
+    sum_send, sum_recv, unit_send, unit_recv, scat_send, scat_recv, line_send, line_recv,
     ring_send, ring_recv, peer_send, peer_recv, score_send, score_recv,
 ):
     sec = lax.axis_index("section")
@@ -151,10 +152,26 @@
                 xg[block, :], wv[:, n:n + 256], preferred_element_type=jnp.float32
             )
 
-    def finish(start, slot, a):
+    def decode(at, chunk, cols):
+        count = landed[at, cols].astype(jnp.int32).astype(jnp.float32)
+        return count * unit_landed[chunk, :, cols]
+
+    def encode(at, chunk, add):
+        for n in range(0, part_sum.shape[1], 256):
+            cols = slice(n, n + 256)
+            value = part_sum[at, cols]
+            if add:
+                value = value + decode(at, chunk, cols)
+            most = jnp.max(jnp.abs(value), axis=0, keepdims=True)
+            most = jnp.maximum(most, 1e-30)
+            unit_sent[chunk, :, cols] = most * (1.0 / STEPS)
+            count = jnp.round(value * (STEPS / most)).astype(jnp.int32)
+            sent[at, cols] = count.astype(jnp.int16)
+
+    def finish(start, slot, a, chunk):
         def some(t, carry):
             at = rows_at(start + t * 16, 16, 16)
-            hidden = part_sum[at, :] + landed[at, :]
+            hidden = part_sum[at, :] + decode(at, chunk, slice(None))
             gate = jax.nn.sigmoid(hidden)
             term = hidden * gate * read_ref[...]
             folded = term[:, 0:128]
@@ -186,25 +203,35 @@
         def _():
             at = rows_at(start, SUB, SUB)
             count = slot * 2 + a
+            chunk = slot * 4 + half * 2 + a
 
             @pl.when(hop > 0)
             def _():
                 wait_for(landed.at[at], sum_recv.at[half, count])
+                wait_for(unit_landed.at[chunk], unit_recv.at[half, count])
+
+            @pl.when(hop == 0)
+            def _():
+                encode(at, chunk, False)
 
             @pl.when((hop > 0) & (hop < LAST))
             def _():
-                part_sum[at, :] = part_sum[at, :] + landed[at, :]
+                encode(at, chunk, True)
 
             @pl.when(hop < LAST)
             def _():
                 push(
-                    part_sum.at[at], landed.at[at], sum_send.at[half],
+                    sent.at[at], landed.at[at], sum_send.at[half],
                     sum_recv.at[half, count], d_=onward,
                 )
+                push(
+                    unit_sent.at[chunk], unit_landed.at[chunk], unit_send.at[half],
+                    unit_recv.at[half, count], d_=onward,
+                )
 
             @pl.when(hop == LAST)
             def _():
-                finish(start, slot, a)
+                finish(start, slot, a, chunk)
 
     def quarter(slot, half, q):
         return slope.at[rows_at(slot * ROWS + half * HALF + q * PIECE, PIECE, PIECE)]
@@ -372,7 +399,8 @@
 
         @pl.when(sum_hop < LAST)
         def _():
-            wait_for(part_sum.at[0:SLOTS * HALF], sum_send.at[half])
+            wait_for(sent.at[0:SLOTS * HALF], sum_send.at[half])
+            wait_for(unit_sent.at[0:SLOTS * 2], unit_send.at[half])
 
         @pl.when(source)
         def _():
@@ -422,7 +450,10 @@
             pltpu.VMEM((tokens, width), jnp.bfloat16),
             pltpu.VMEM((width, units), jnp.bfloat16),
             pltpu.VMEM((tokens, units), jnp.float32),
-            pltpu.VMEM((tokens, units), jnp.float32),
+            pltpu.VMEM((tokens, units), jnp.int16),
+            pltpu.VMEM((tokens, units), jnp.int16),
+            pltpu.VMEM((4 * SLOTS, 1, units), jnp.float32),
+            pltpu.VMEM((4 * SLOTS, 1, units), jnp.float32),
             pltpu.VMEM((tokens, units), jnp.bfloat16),
             pltpu.VMEM((128, 128), jnp.float32),
             pltpu.VMEM((8, 128), jnp.float32),
@@ -431,7 +462,7 @@
             pltpu.VMEM((8, 128), jnp.float32),
             pltpu.VMEM((8, 8, 128), jnp.float32),
             dma((2,)), dma((2,)), dma, dma, dma((2, 3)), dma((8, 4)), dma((8, 4)),
-            dma((2,)), dma((2, 16)), dma((2,)), dma((2, 8)), dma((2,)), dma((2, 8)),
+            dma((2,)), dma((2, 16)), dma((2,)), dma((2, 16)), dma((2,)), dma((2, 8)), dma((2,)), dma((2, 8)),
             dma((2,)), dma((2, 8, 3)), dma, dma, dma, dma,
         ],
         compiler_params=pltpu.CompilerParams(

time: 185 us -> 139 us (0.75)
  Pallas kernels: 168 us -> 122 us
    pallas_call x1, Pallas kernels: 168 us -> 122 us  [score_and_slope(): pl.pallas_call(slab_kernel, out_shape=(jax.ShapeDtypeStruct((8, 8, 128),...]
where the time goes in v2:
time: 139 us
  Pallas kernels  122 us (88%)
  matrix products  8.36 us (6%)
  other arithmetic  3.1 us (2%)
  local copies, waits for them, and re-layouts  2.99 us (2%)
  between operations  2.51 us (2%)
    pallas_call x1, Pallas kernels, score_and_slope(): pl.pallas_call(slab_kernel, out_shape=(jax.ShapeDtypeStruct((8, 8, 128),...  122 us
    dot_general x2, matrix products, contract_rows(): lax.dot_general(left, right, (((0,), (0,)), ((), ())), preferred_element_...  8.36 us

profile of v2, /device:TPU:6, one launch (start us, length us, event | category | flops | bytes accessed | tf_op | source)
XLA Modules:
  0.0 138.9 jit_solution(8098902634484377041)
XLA Ops:
  0.6 0.0 copy-start.2
  0.7 0.7 compare_and_fusion.1
  1.4 0.7 copy.11
  2.1 0.1 reduce.1
  2.3 0.7 fusion.33
  3.0 0.1 multiply_add_fusion
  3.1 0.1 reshape.138
  3.2 0.0 copy-start
  3.2 0.9 copy-done
  4.1 0.0 copy-start.1
  4.1 0.7 copy-done.1
  4.8 121.9 %score_and_slope.1 = (f32[8,8,128]{2,1,0:T(8,128)S(1)}, bf16[2048,1024]{1,0:T(8,128)(2,1)}, bf16[2048,512]{1,0:T(8,128)(2,1)S(1)}) custom-call(bf16[32,2048]{1,0:T(8,128)(2,1)S(1)} %copy-done, bf16[1,2048,1024]{2,1,0:T(8,128)(2,1)} %w_hbm.1, f32[1,1024]{1,0:T(1,128)S(1)} %copy-done.1), custom_call_target="tpu_custom_call" | custom-call | tf_op jit(solution)/shard_map/score_and_slope/pallas_call | solution.py:440
  126.7 0.2 select_reduce_fusion.1
  126.9 0.0 copy-done.2
  126.9 0.2 fusion.17
  127.1 0.2 fusion.18
  127.3 0.1 select_reduce_fusion
  127.4 0.6 fusion.28
  128.7 0.6 gather_fusion
  129.3 0.1 select_bitcast_fusion
  129.4 0.0 copy-start.3
  129.4 4.9 %fusion.1 = f32[512,1024]{1,0:T(8,128)S(1)} fusion(bf16[2048,512]{1,0:T(8,128)(2,1)S(1)} %get-tuple-element.5, bf16[2048,1024]{1,0:T(8,128)(2,1)} %get-tuple-element.7, f32[2048]{0:T(1024)S(1)} %bitcast.29), kind=kOutput, calls=%fused_computation.4 | convolution fusion | flops 2153775104 | bytes 8396800 | tf_op jit(solution)/shard_map/dot_general | solution.py:484
  134.2 0.0 copy-done.3
  134.2 3.5 %fusion.6 = bf16[1,512,1024]{2,1,0:T(8,128)(2,1)} fusion(f32[512,1024]{1,0:T(8,128)S(1)} %fusion.1, bf16[2048,512]{1,0:T(8,128)(2,1)S(1)} %get-tuple-element.5, bf16[2048,1024]{1,0:T(8,128)(2,1)S(1)} %copy-done.3, f32[2048]{0:T(1024)S(1)} %bitcast.30), kind=kOutput, calls=%fused_computation.9 | convolution fusion | flops 2161115136 | bytes 9445376 | tf_op jit(solution)/shard_map/dot_general | solution.py:484
  (7 shorter events, 0.1 us)
Async XLA Ops:
  0.6 126.3 %copy-start.2 = (s32[16]{0:T(128)S(1)}, s32[16]{0:T(128)}, u32[]{:S(2)}) copy-start(s32[16]{0:T(128)} %param.11) | copy-start | bytes 196
  3.2 0.9 copy-start
  4.1 0.7 copy-start.1
  129.4 4.9 %copy-start.3 = (bf16[2048,1024]{1,0:T(8,128)(2,1)S(1)}, bf16[2048,1024]{1,0:T(8,128)(2,1)}, u32[]{:S(2)}) copy-start(bf16[2048,1024]{1,0:T(8,128)(2,1)} %get-tuple-element.7) | copy-start | bytes 12582916

commit v3 on v2

--- a/solution.py
+++ b/solution.py
@@ -528,10 +528,8 @@
     )
     by_block = coeff.reshape(2, SLOTS, HALF).transpose(1, 0, 2).reshape(SLOTS, ROWS)
     ordered = jnp.take(by_block, block, axis=0).reshape(total_rows)
-    hidden_grad = ordered[:, None] * slope.astype(jnp.float32)
-    upper = hidden_grad.astype(jnp.bfloat16)
-    lower = (hidden_grad - upper.astype(jnp.float32)).astype(jnp.bfloat16)
-    weight_grad = contract_rows(features, upper) + contract_rows(features, lower)
+    hidden_grad = (ordered[:, None] * slope.astype(jnp.float32)).astype(jnp.bfloat16)
+    weight_grad = contract_rows(features, hidden_grad)
     return (weight_grad.astype(jnp.bfloat16)[None], policy_loss)
 
 

time: 139 us -> 136 us (0.978)
  matrix products: 8.36 us -> 5.69 us
    dot_general x2 -> x1, matrix products: 8.36 us -> 5.69 us  [contract_rows(): lax.dot_general(left, right, (((0,), (0,)), ((), ())), preferred_element_...]
where the time goes in v3:
time: 136 us
  Pallas kernels  122 us (90%)
  matrix products  5.69 us (4%)
  other arithmetic  3.1 us (2%)
  local copies, waits for them, and re-layouts  2.98 us (2%)
  between operations  2.5 us (2%)
    pallas_call x1, Pallas kernels, score_and_slope(): pl.pallas_call(slab_kernel, out_shape=(jax.ShapeDtypeStruct((8, 8, 128),...  122 us
    dot_general x1, matrix products, contract_rows(): lax.dot_general(left, right, (((0,), (0,)), ((), ())), preferred_element_...  5.69 us

profile of v3, /device:TPU:6, one launch (start us, length us, event | category | flops | bytes accessed | tf_op | source)
XLA Modules:
  0.0 136.2 jit_solution(2006497322144652362)
XLA Ops:
  0.6 0.0 copy-start.2
  0.7 0.7 compare_and_fusion.1
  1.4 0.7 copy.11
  2.1 0.1 reduce.1
  2.3 0.7 fusion.30
  3.0 0.1 multiply_add_fusion
  3.1 0.1 reshape.138
  3.2 0.0 copy-start
  3.2 0.9 copy-done
  4.1 0.0 copy-start.1
  4.1 0.7 copy-done.1
  4.8 121.9 %score_and_slope.1 = (f32[8,8,128]{2,1,0:T(8,128)S(1)}, bf16[2048,1024]{1,0:T(8,128)(2,1)}, bf16[2048,512]{1,0:T(8,128)(2,1)S(1)}) custom-call(bf16[32,2048]{1,0:T(8,128)(2,1)S(1)} %copy-done, bf16[1,2048,1024]{2,1,0:T(8,128)(2,1)} %w_hbm.1, f32[1,1024]{1,0:T(1,128)S(1)} %copy-done.1), custom_call_target="tpu_custom_call" | custom-call | tf_op jit(solution)/shard_map/score_and_slope/pallas_call | solution.py:440
  126.7 0.2 select_reduce_fusion.1
  126.9 0.0 copy-done.2
  126.9 0.2 fusion.14
  127.1 0.2 fusion.15
  127.3 0.1 select_reduce_fusion
  127.4 0.6 fusion.25
  128.7 0.6 gather_fusion
  129.3 0.1 select_bitcast_fusion
  129.4 5.7 %fusion.3 = bf16[1,512,1024]{2,1,0:T(8,128)(2,1)} fusion(bf16[2048,512]{1,0:T(8,128)(2,1)S(1)} %get-tuple-element.5, bf16[2048,1024]{1,0:T(8,128)(2,1)} %get-tuple-element.7, f32[2048]{0:T(1024)S(1)} %bitcast.28), kind=kOutput, calls=%fused_computation.5 | convolution fusion | flops 2154299392 | bytes 7348224 | tf_op jit(solution)/shard_map/dot_general | solution.py:484
  (7 shorter events, 0.1 us)
Async XLA Ops:
  0.6 126.3 %copy-start.2 = (s32[16]{0:T(128)S(1)}, s32[16]{0:T(128)}, u32[]{:S(2)}) copy-start(s32[16]{0:T(128)} %param.11) | copy-start | bytes 196
  3.2 0.9 copy-start
  4.1 0.7 copy-start.1
